TPU v7x, 32 devices: a whole 2x2x4 slice. The times are simulated.
32 devices in a mesh: ctx: 8 (over z, x), wt: 4 (over y, core).
Axes of the slice: x: 2, y: 2, z: 4, core: 2. Of those that a mesh axis runs over, the one named last changes fastest.
Arguments:
- hidden_in: bfloat16 [2, 4, 1024, 960], P(None, 'wt', 'ctx'), may hold values from -6 to 6
- d_out: bfloat16 [2, 4, 1024, 960], P(None, 'wt', 'ctx'), may hold values from -6 to 6
- block_order: int32 [2, 16], replicated, may hold values from 0 to 15, as said below
- gain_attn: bfloat16 [960], P('wt'), may hold values from 0.5 to 1.5
- gain_mlp: bfloat16 [960], P('wt'), may hold values from 0.5 to 1.5
- w_q: bfloat16 [960, 960], P('wt'), may hold values from -0.25 to 0.25
- w_kv: bfloat16 [960, 640], P('wt'), may hold values from -0.1875 to 0.1875
- w_o: bfloat16 [960, 960], P('wt'), may hold values from -3 to 3
- w_gu: bfloat16 [960, 5120], P('wt'), may hold values from -0.1875 to 0.1875
- w_down: bfloat16 [2560, 960], P('wt'), may hold values from -0.25 to 0.25
Outputs:
- hidden_out: bfloat16 [2, 4, 1024, 960], P(None, 'wt', 'ctx')
- grad_in: bfloat16 [2, 4, 1024, 960], P(None, 'wt', 'ctx')
- grad_gain_attn: float32 [960], P('wt')
- grad_gain_mlp: float32 [960], P('wt')
- grad_w_q: float32 [960, 960], P('wt')
- grad_w_kv: float32 [960, 640], P('wt')
- grad_w_o: float32 [960, 960], P('wt')
- grad_w_gu: float32 [960, 5120], P('wt')
- grad_w_down: float32 [2560, 960], P('wt')
Inputs may be any that keep to these rules, and one draw needn't show every extreme that they name: block_order[m] is a permutation of the 16 blocks in which stored blocks 2c and 2c + 1 are a mirrored pair: their numbers add up to 15.
All inputs are finite; a program needn't handle non-finite values.
Results may differ from a plain program's by a relative error of at most 0.018.
Values may be sent and summed in bfloat16 or wider, within the bound.
A program may use at most 256 MiB of HBM per device.

v0:
```python
import math
import jax
import jax.numpy as jnp
from jax import lax
from jax.sharding import PartitionSpec as P

QH = 15
KVH = 5
HD = 64
eps_norm = 1e-05
rope_base = 10000.0


def norm_scale(values, gain):
    return values * lax.rsqrt(jnp.mean(values * values, axis=-1, keepdims=True) + eps_norm) * gain


def rope_tables(positions):
    half_dim = HD // 2
    frequency = jnp.exp(jnp.arange(half_dim, dtype=jnp.float32) * (-2.0 * math.log(rope_base) / HD))
    angles = positions.astype(jnp.float32)[:, None] * frequency[None, :]
    return (jnp.cos(angles), jnp.sin(angles))


def rotate(values, cosine, sine):
    half_dim = values.shape[-1] // 2
    first_half = values[..., :half_dim]
    second_half = values[..., half_dim:]
    cos_wide = cosine[:, None, :]
    sin_wide = sine[:, None, :]
    return jnp.concatenate(
        [
            first_half * cos_wide - second_half * sin_wide,
            second_half * cos_wide + first_half * sin_wide,
        ],
        axis=-1,
    )


def unrotate(values, cosine, sine):
    half_dim = values.shape[-1] // 2
    first_half = values[..., :half_dim]
    second_half = values[..., half_dim:]
    cos_wide = cosine[:, None, :]
    sin_wide = sine[:, None, :]
    return jnp.concatenate(
        [
            first_half * cos_wide + second_half * sin_wide,
            second_half * cos_wide - first_half * sin_wide,
        ],
        axis=-1,
    )


def block_size(total_rows, limit):
    best_size = 1
    for candidate in range(1, min(total_rows, limit) + 1):
        if total_rows % candidate == 0:
            best_size = candidate
    return best_size


def outer_sum(left, right):
    return lax.dot_general(
        left, right, (((0,), (0,)), ((), ())), preferred_element_type=jnp.float32
    )


def back_product(left, weight):
    return lax.dot_general(
        left, weight, (((1,), (1,)), ((), ())), preferred_element_type=jnp.float32
    )


def block_scores(query_groups, keys_block, key_pos, row_pos, score_scale):
    scores = (
        jnp.einsum("hrd,khd->hrk", query_groups, keys_block, preferred_element_type=jnp.float32)
        * score_scale
    )
    visible = key_pos[None, None, :] <= row_pos[None, :, None]
    return (scores, visible)


def local(hidden_in, d_out, block_order, gain_attn, gain_mlp, w_q, w_kv, w_o, w_gu, w_down):
    gathered = (
        lax.all_gather(gain_attn, "wt", axis=0, tiled=True),
        lax.all_gather(gain_mlp, "wt", axis=0, tiled=True),
        lax.all_gather(w_q, "wt", axis=0, tiled=True),
        lax.all_gather(w_kv, "wt", axis=0, tiled=True),
        lax.all_gather(w_o, "wt", axis=0, tiled=True),
        lax.all_gather(w_gu, "wt", axis=0, tiled=True),
        lax.all_gather(w_down, "wt", axis=0, tiled=True),
    )
    gain_one = gathered[0].astype(jnp.float32)
    gain_two = gathered[1].astype(jnp.float32)
    weight_q, weight_kv, weight_o, weight_gu, weight_down = (
        gathered[2],
        gathered[3],
        gathered[4],
        gathered[5],
        gathered[6],
    )
    micro_count = hidden_in.shape[0]
    seg_rows = hidden_in.shape[2]
    n_ctx = lax.axis_size("ctx")
    seq_len = seg_rows * n_ctx
    half_block = seg_rows // 2
    kv_width = KVH * HD
    group_size = QH // KVH
    row_count = group_size * seg_rows
    ff_width = weight_down.shape[0]
    key_block = block_size(seq_len, 1024)
    block_count = seq_len // key_block
    score_scale = 1.0 / math.sqrt(HD)
    my_start = lax.axis_index("ctx") * seg_rows
    grad_names = [jnp.zeros(item.shape, jnp.float32) for item in gathered]
    outputs = []
    input_grads = []
    for micro_index in range(micro_count):
        tokens_in = hidden_in[micro_index, 0].astype(jnp.float32)
        order_row = block_order[micro_index]
        key_pos = (
            order_row[:, None] * half_block + jnp.arange(half_block, dtype=jnp.int32)[None, :]
        ).reshape(seq_len)
        query_pos = lax.dynamic_slice_in_dim(key_pos, my_start, seg_rows)
        row_pos = jnp.tile(query_pos, group_size)
        cosine, sine = rope_tables(query_pos)
        normed_one, pull_one = jax.vjp(norm_scale, tokens_in, gain_one)
        act_one = normed_one.astype(jnp.bfloat16)
        query_lin = jnp.dot(act_one, weight_q, preferred_element_type=jnp.float32).reshape(
            seg_rows, QH, HD
        )
        query_rot = rotate(query_lin, cosine, sine).astype(jnp.bfloat16)
        query_groups = (
            query_rot.reshape(seg_rows, KVH, group_size, HD)
            .transpose(1, 2, 0, 3)
            .reshape(KVH, row_count, HD)
        )
        kv_lin = jnp.dot(act_one, weight_kv, preferred_element_type=jnp.float32)
        key_rot = rotate(kv_lin[:, :kv_width].reshape(seg_rows, KVH, HD), cosine, sine).reshape(
            seg_rows, kv_width
        )
        kv_send = jnp.concatenate([key_rot, kv_lin[:, kv_width:]], axis=1).astype(jnp.bfloat16)
        kv_whole = lax.all_gather(kv_send, "ctx", axis=0, tiled=True)
        kv_blocks = kv_whole.reshape(block_count, key_block, 2 * kv_width)
        pos_blocks = key_pos.reshape(block_count, key_block)

        def lse_step(carry, item):
            top_now, total_now = carry
            kv_block, kpos = item
            keys_block = kv_block[:, :kv_width].reshape(key_block, KVH, HD)
            scores, visible = block_scores(query_groups, keys_block, kpos, row_pos, score_scale)
            top_new = jnp.maximum(top_now, jnp.max(jnp.where(visible, scores, -1e30), axis=-1))
            total_new = total_now * jnp.exp(top_now - top_new) + jnp.sum(
                jnp.where(visible, jnp.exp(scores - top_new[..., None]), 0.0), axis=-1
            )
            return ((top_new, total_new), None)

        start_top = jnp.full((KVH, row_count), -1e30, jnp.float32)
        start_total = jnp.zeros((KVH, row_count), jnp.float32)
        (top_all, total_all), _ = lax.scan(
            lse_step, (start_top, start_total), (kv_blocks, pos_blocks)
        )
        lse = top_all + jnp.log(total_all)

        def value_step(acc_now, item):
            kv_block, kpos = item
            keys_block = kv_block[:, :kv_width].reshape(key_block, KVH, HD)
            vals_block = kv_block[:, kv_width:].reshape(key_block, KVH, HD)
            scores, visible = block_scores(query_groups, keys_block, kpos, row_pos, score_scale)
            probs = jnp.where(visible, jnp.exp(scores - lse[..., None]), 0.0).astype(jnp.bfloat16)
            return (
                acc_now
                + jnp.einsum("hrk,khd->hrd", probs, vals_block, preferred_element_type=jnp.float32),
                None,
            )

        acc_all, _ = lax.scan(
            value_step, jnp.zeros((KVH, row_count, HD), jnp.float32), (kv_blocks, pos_blocks)
        )
        attn_low = (
            acc_all.reshape(KVH, group_size, seg_rows, HD)
            .transpose(2, 0, 1, 3)
            .reshape(seg_rows, QH * HD)
            .astype(jnp.bfloat16)
        )
        mid_state = tokens_in + jnp.dot(attn_low, weight_o, preferred_element_type=jnp.float32)
        normed_two, pull_two = jax.vjp(norm_scale, mid_state, gain_two)
        act_two = normed_two.astype(jnp.bfloat16)
        gate_up = jnp.dot(act_two, weight_gu, preferred_element_type=jnp.float32)
        gate_part = gate_up[:, :ff_width]
        up_part = gate_up[:, ff_width:]
        sig_gate = jax.nn.sigmoid(gate_part)
        hidden_low = (gate_part * sig_gate * up_part).astype(jnp.bfloat16)
        result = mid_state + jnp.dot(hidden_low, weight_down, preferred_element_type=jnp.float32)
        outputs.append(result.astype(jnp.bfloat16))
        grad_low = d_out[micro_index, 0]
        grad_top = grad_low.astype(jnp.float32)
        grad_down = outer_sum(hidden_low, grad_low)
        d_hidden = back_product(grad_low, weight_down)
        d_gate = d_hidden * up_part * sig_gate * (1.0 + gate_part * (1.0 - sig_gate))
        d_up = d_hidden * gate_part * sig_gate
        d_gu_low = jnp.concatenate([d_gate, d_up], axis=1).astype(jnp.bfloat16)
        grad_gu = outer_sum(act_two, d_gu_low)
        d_act_two = back_product(d_gu_low, weight_gu)
        d_mid_norm, grad_gain_two = pull_two(d_act_two)
        d_mid = grad_top + d_mid_norm
        d_mid_low = d_mid.astype(jnp.bfloat16)
        grad_o = outer_sum(attn_low, d_mid_low)
        d_attn_low = back_product(d_mid_low, weight_o).astype(jnp.bfloat16)
        grad_groups = (
            d_attn_low.reshape(seg_rows, KVH, group_size, HD)
            .transpose(1, 2, 0, 3)
            .reshape(KVH, row_count, HD)
        )
        kv_back = lax.all_gather(kv_send, "ctx", axis=0, tiled=True).reshape(
            block_count, key_block, 2 * kv_width
        )

        def delta_step(delta_now, item):
            kv_block, kpos = item
            keys_block = kv_block[:, :kv_width].reshape(key_block, KVH, HD)
            vals_block = kv_block[:, kv_width:].reshape(key_block, KVH, HD)
            scores, visible = block_scores(query_groups, keys_block, kpos, row_pos, score_scale)
            probs = jnp.where(visible, jnp.exp(scores - lse[..., None]), 0.0)
            d_probs = jnp.einsum(
                "hrd,khd->hrk", grad_groups, vals_block, preferred_element_type=jnp.float32
            )
            return (delta_now + jnp.sum(probs * d_probs, axis=-1), None)

        delta, _ = lax.scan(
            delta_step, jnp.zeros((KVH, row_count), jnp.float32), (kv_back, pos_blocks)
        )

        def grad_step(dq_now, item):
            kv_block, kpos = item
            keys_block = kv_block[:, :kv_width].reshape(key_block, KVH, HD)
            vals_block = kv_block[:, kv_width:].reshape(key_block, KVH, HD)
            scores, visible = block_scores(query_groups, keys_block, kpos, row_pos, score_scale)
            probs = jnp.where(visible, jnp.exp(scores - lse[..., None]), 0.0)
            d_probs = jnp.einsum(
                "hrd,khd->hrk", grad_groups, vals_block, preferred_element_type=jnp.float32
            )
            d_scores = (probs * (d_probs - delta[..., None])).astype(jnp.bfloat16)
            dq_new = dq_now + jnp.einsum(
                "hrk,khd->hrd", d_scores, keys_block, preferred_element_type=jnp.float32
            )
            d_keys = (
                jnp.einsum(
                    "hrk,hrd->khd", d_scores, query_groups, preferred_element_type=jnp.float32
                )
                * score_scale
            )
            d_vals = jnp.einsum(
                "hrk,hrd->khd",
                probs.astype(jnp.bfloat16),
                grad_groups,
                preferred_element_type=jnp.float32,
            )
            return (
                dq_new,
                jnp.concatenate(
                    [d_keys.reshape(key_block, kv_width), d_vals.reshape(key_block, kv_width)],
                    axis=1,
                ),
            )

        dq_groups, dkv_blocks = lax.scan(
            grad_step, jnp.zeros((KVH, row_count, HD), jnp.float32), (kv_back, pos_blocks)
        )
        dkv_mine = lax.psum_scatter(
            dkv_blocks.reshape(seq_len, 2 * kv_width), "ctx", scatter_dimension=0, tiled=True
        )
        d_query = (
            (dq_groups * score_scale)
            .reshape(KVH, group_size, seg_rows, HD)
            .transpose(2, 0, 1, 3)
            .reshape(seg_rows, QH, HD)
        )
        d_q_low = unrotate(d_query, cosine, sine).reshape(seg_rows, QH * HD).astype(jnp.bfloat16)
        d_key = unrotate(dkv_mine[:, :kv_width].reshape(seg_rows, KVH, HD), cosine, sine).reshape(
            seg_rows, kv_width
        )
        d_kv_low = jnp.concatenate([d_key, dkv_mine[:, kv_width:]], axis=1).astype(jnp.bfloat16)
        grad_q = outer_sum(act_one, d_q_low)
        grad_kv = outer_sum(act_one, d_kv_low)
        d_act_one = back_product(d_q_low, weight_q) + back_product(d_kv_low, weight_kv)
        d_in_norm, grad_gain_one = pull_one(d_act_one)
        input_grads.append((d_mid + d_in_norm).astype(jnp.bfloat16))
        parts_now = [grad_gain_one, grad_gain_two, grad_q, grad_kv, grad_o, grad_gu, grad_down]
        grad_names = [total + piece for total, piece in zip(grad_names, parts_now)]
    owned = (
        lax.psum_scatter(
            grad_names[0].astype(jnp.bfloat16), "wt", scatter_dimension=0, tiled=True
        ).astype(jnp.float32),
        lax.psum_scatter(
            grad_names[1].astype(jnp.bfloat16), "wt", scatter_dimension=0, tiled=True
        ).astype(jnp.float32),
        lax.psum_scatter(
            grad_names[2].astype(jnp.bfloat16), "wt", scatter_dimension=0, tiled=True
        ).astype(jnp.float32),
        lax.psum_scatter(
            grad_names[3].astype(jnp.bfloat16), "wt", scatter_dimension=0, tiled=True
        ).astype(jnp.float32),
        lax.psum_scatter(
            grad_names[4].astype(jnp.bfloat16), "wt", scatter_dimension=0, tiled=True
        ).astype(jnp.float32),
        lax.psum_scatter(
            grad_names[5].astype(jnp.bfloat16), "wt", scatter_dimension=0, tiled=True
        ).astype(jnp.float32),
        lax.psum_scatter(
            grad_names[6].astype(jnp.bfloat16), "wt", scatter_dimension=0, tiled=True
        ).astype(jnp.float32),
    )
    summed = lax.psum((owned[0], owned[1], owned[2], owned[3], owned[4], owned[5], owned[6]), "ctx")
    hidden_out = jnp.stack(outputs)[:, None]
    grad_in = jnp.stack(input_grads)[:, None]
    return (
        hidden_out,
        grad_in,
        summed[0],
        summed[1],
        summed[2],
        summed[3],
        summed[4],
        summed[5],
        summed[6],
    )


def solution(mesh):
    placed = (
        P(None, "wt", "ctx", None),
        P(None, "wt", "ctx", None),
        P(),
        P("wt"),
        P("wt"),
        P("wt", None),
        P("wt", None),
        P("wt", None),
        P("wt", None),
        P("wt", None),
    )
    return jax.shard_map(
        local,
        mesh=mesh,
        in_specs=placed,
        out_specs=(
            P(None, "wt", "ctx", None),
            P(None, "wt", "ctx", None),
            P("wt"),
            P("wt"),
            P("wt", None),
            P("wt", None),
            P("wt", None),
            P("wt", None),
            P("wt", None),
        ),
        check_vma=False,
    )
```

profile of v0, /device:TPU:0, one launch (start us, length us, event | category | flops | bytes accessed | tf_op | source)
XLA Modules:
  0.0 1084.1 jit_solution(5646645169143521290)
XLA Ops:
  12.4 8.3 all-reduce.6
  23.4 6.6 all-gather.10.cloned.1.call-done
  37.8 15.7 %all-gather.8.cloned.1.call-done = bf16[960,960]{1,0:T(8,128)(2,1)} async-done(((bf16[240,960]{1,0:T(8,128)(2,1)}), bf16[960,960]{1,0:T(8,128)(2,1)}) %all-gather.8.cloned.1.call-update) | async-done | bytes 1843216 | tf_op jit(solution)/shard_map/all_gather | solution.py:88
  59.6 38.7 %all-gather.20.cloned.1.call-done = bf16[1024,640]{1,0:T(8,128)(2,1)} async-done(((bf16[128,640]{1,0:T(8,128)(2,1)}), bf16[1024,640]{1,0:T(8,128)(2,1)}) %all-gather.20.cloned.1.call-update) | async-done | bytes 1310736 | tf_op jit(solution)/shard_map/all_gather | solution.py:144
  110.2 31.5 %all-gather.12.cloned.1.call-done = bf16[1024,640]{1,0:T(8,128)(2,1)} async-done(((bf16[128,640]{1,0:T(8,128)(2,1)}), bf16[1024,640]{1,0:T(8,128)(2,1)}) %all-gather.12.cloned.1.call-update) | async-done | bytes 1310736 | tf_op jit(solution)/shard_map/all_gather | solution.py:144
  152.6 11.0 %all-gather.14.cloned.1.call-done = bf16[960,960]{1,0:T(8,128)(2,1)} async-done(((bf16[240,960]{1,0:T(8,128)(2,1)}), bf16[960,960]{1,0:T(8,128)(2,1)}) %all-gather.14.cloned.1.call-update) | async-done | bytes 1843216 | tf_op jit(solution)/shard_map/all_gather | solution.py:90
  168.5 63.0 %all-gather.16.cloned.1.call-done = bf16[960,5120]{1,0:T(8,128)(2,1)} async-done(((bf16[240,5120]{1,0:T(8,128)(2,1)}), bf16[960,5120]{1,0:T(8,128)(2,1)}) %all-gather.16.cloned.1.call-update) | async-done | bytes 9830416 | tf_op jit(solution)/shard_map/all_gather | solution.py:91
  231.6 7.1 fusion.88
  241.8 29.9 %all-gather.18.cloned.1.call-done = bf16[2560,960]{0,1:T(8,128)(2,1)} async-done(((bf16[640,960]{0,1:T(8,128)(2,1)}), bf16[2560,960]{0,1:T(8,128)(2,1)}) %all-gather.18.cloned.1.call-update) | async-done | bytes 4915216 | tf_op jit(solution)/shard_map/all_gather | solution.py:92
  271.7 5.5 multiply_convert_fusion.3
  277.2 5.2 multiply_convert_fusion.5
  294.3 6.6 multiply_reduce_fusion
  300.9 5.1 fusion.89
  306.0 4.5 multiply_convert_fusion
  317.3 6.8 multiply_reduce_fusion.1
  324.1 4.6 multiply_convert_fusion.1
  333.5 3.5 convolution_multiply_fusion.2
  337.3 4.3 convolution_multiply_fusion.3
  349.1 37.0 %reduce-scatter.12.cloned.1.call-done = f32[128,640]{0,1:T(8,128)} async-done(((f32[1024,640]{0,1:T(8,128)}), f32[128,640]{0,1:T(8,128)}) %reduce-scatter.12.cloned.1.call-update) | async-done | bytes 327696 | tf_op jit(solution)/shard_map/reduce_scatter | solution.py:271
  388.0 71.2 %reduce-scatter.10.cloned.1.call-done = f32[128,640]{0,1:T(8,128)} async-done(((f32[1024,640]{0,1:T(8,128)}), f32[128,640]{0,1:T(8,128)}) %reduce-scatter.10.cloned.1.call-update) | async-done | bytes 327696 | tf_op jit(solution)/shard_map/reduce_scatter | solution.py:271
  466.4 3.7 add_convert_fusion.1
  470.1 7.9 copy.86
  478.0 9.6 fusion.7
  487.6 11.8 %add_convert_fusion = bf16[960,5120]{1,0:T(8,128)(2,1)} fusion(f32[960,5120]{1,0:T(8,128)} %fusion.7, bf16[128,2560]{1,0:T(8,128)(2,1)} %copy-done.46, bf16[128,2560]{1,0:T(8,128)(2,1)} %copy-done.45, f32[128,960]{0,1:T(8,128)S(1)} %get-tuple-element.300, f32[128]{0:T(128)S(1)} %fusion.78, f32[960]{0:T(1024)S(1)} %convert_element_type.227), kind=kOutput, calls=%fused_computation | convolution fusion | flops 1271111680 | bytes 31297792 | tf_op jit(solution)/shard_map/dot_general | solution.py:64
  500.1 4.1 fusion.4
  504.3 4.2 fusion.5
  512.3 12.9 %reduce-scatter.18.cloned.1.call-done = bf16[240,960]{1,0:T(8,128)(2,1)} async-done(((bf16[960,960]{1,0:T(8,128)(2,1)}), bf16[240,960]{1,0:T(8,128)(2,1)}) %reduce-scatter.18.cloned.1.call-update) | async-done | bytes 460816 | tf_op jit(solution)/shard_map/reduce_scatter | solution.py:305
  529.2 5.7 all-reduce.5
  537.3 16.5 %reduce-scatter.16.cloned.1.call-done = bf16[240,640]{1,0:T(8,128)(2,1)} async-done(((bf16[960,640]{1,0:T(8,128)(2,1)}), bf16[240,640]{1,0:T(8,128)(2,1)}) %reduce-scatter.16.cloned.1.call-update) | async-done | bytes 307216 | tf_op jit(solution)/shard_map/reduce_scatter | solution.py:302
  553.8 54.1 %reduce-scatter.22.cloned.1.call-done = bf16[640,960]{1,0:T(8,128)(2,1)} async-done(((bf16[2560,960]{1,0:T(8,128)(2,1)}), bf16[640,960]{1,0:T(8,128)(2,1)}) %reduce-scatter.22.cloned.1.call-update) | async-done | bytes 1228816
  610.0 81.4 %reduce-scatter.20.cloned.1.call-done = bf16[240,5120]{1,0:T(8,128)(2,1)} async-done(((bf16[960,5120]{1,0:T(8,128)(2,1)}), bf16[240,5120]{1,0:T(8,128)(2,1)}) %reduce-scatter.20.cloned.1.call-update) | async-done | bytes 2457616 | tf_op jit(solution)/shard_map/reduce_scatter | solution.py:308
  691.4 385.8 %all-reduce.8 = (f32[240]{0:T(256)}, f32[240]{0:T(256)}, f32[240,960]{1,0:T(8,128)}, f32[240,640]{1,0:T(8,128)}, f32[240,960]{1,0:T(8,128)}, /*index=5*/f32[240,5120]{1,0:T(8,128)}, f32[640,960]{0,1:T(8,128)}) all-reduce(f32[240]{0:T(256)S(1)} %get-tuple-element.314, ...), channel_id=1, replica_groups=mesh['ctx'=8,'wt'=4] {'ctx'}, use_global_device_ids=true, to_apply=%region_19.20 | all-reduce | flops 2458080 | bytes 14749440 | tf_op jit(solution)/shard_map/psum | solution.py:315
  (299 shorter events, 103.1 us)
Async XLA Ops:
  7.2 26.2 %copy-start.6 = (bf16[2,1,128,960]{2,3,1,0:T(8,128)(2,1)S(1)}, bf16[2,1,128,960]{2,3,1,0:T(8,128)(2,1)}, u32[]{:S(2)}) copy-start(bf16[2,1,128,960]{2,3,1,0:T(8,128)(2,1)} %param.10) | copy-start | bytes 1474564
  7.2 22.9 %all-gather.10.cloned.1.call-start = ((), (), s32[]{:S(2)}) async-start(), calls=%async_computation.8 | async-start | bytes 1536000 | tf_op jit(solution)/shard_map/all_gather | solution.py:89
  7.9 45.6 %all-gather.8.cloned.1.call-start = ((), (), s32[]{:S(2)}) async-start(), calls=%async_computation.7 | async-start | bytes 2457600 | tf_op jit(solution)/shard_map/all_gather | solution.py:88
  8.7 89.7 %all-gather.20.cloned.1.call-start = ((), (), s32[]{:S(2)}) async-start(), calls=%async_computation.13 | async-start | bytes 1474560 | tf_op jit(solution)/shard_map/all_gather | solution.py:144
  23.2 12.0 %copy-start.63 = (f32[128]{0:T(128)}, f32[128]{0:T(128)S(1)}, u32[]{:S(2)}) copy-start(f32[128]{0:T(128)S(1)} %get-tuple-element.219) | copy-start | bytes 1540
  23.4 34.7 %copy-start.49 = (f32[128,32]{0,1:T(8,128)}, f32[128,32]{0,1:T(8,128)S(1)}, u32[]{:S(2)}) copy-start(f32[128,32]{0,1:T(8,128)S(1)} %get-tuple-element.295) | copy-start | bytes 49156
  23.4 34.7 %copy-start.51 = (f32[128,32]{0,1:T(8,128)}, f32[128,32]{0,1:T(8,128)S(1)}, u32[]{:S(2)}) copy-start(f32[128,32]{0,1:T(8,128)S(1)} %get-tuple-element.296) | copy-start | bytes 49156
  33.3 108.4 %all-gather.12.cloned.1.call-start = ((), (), s32[]{:S(2)}) async-start(), calls=%async_computation.9 | async-start | bytes 1474560 | tf_op jit(solution)/shard_map/all_gather | solution.py:144
  35.2 128.5 %all-gather.14.cloned.1.call-start = ((), (), s32[]{:S(2)}) async-start(), calls=%async_computation.10 | async-start | bytes 2457600 | tf_op jit(solution)/shard_map/all_gather | solution.py:90
  35.8 195.8 %all-gather.16.cloned.1.call-start = ((), (), s32[]{:S(2)}) async-start(), calls=%async_computation.11 | async-start | bytes 12288000 | tf_op jit(solution)/shard_map/all_gather | solution.py:91
  36.4 235.3 %all-gather.18.cloned.1.call-start = ((), (), s32[]{:S(2)}) async-start(), calls=%async_computation.12 | async-start | bytes 6144000 | tf_op jit(solution)/shard_map/all_gather | solution.py:92
  37.1 349.0 %reduce-scatter.12.cloned.1.call-start = ((), (), s32[]{:S(2)}) async-start(), calls=%async_computation.15 | async-start | bytes 2949120 | tf_op jit(solution)/shard_map/reduce_scatter | solution.py:271
  37.5 70.0 %copy-start.12 = (pred[384,1024]{1,0:T(8,128)(4,1)}, pred[384,1024]{1,0:T(8,128)(4,1)S(1)}, u32[]{:S(2)}) copy-start(pred[384,1024]{1,0:T(8,128)(4,1)S(1)} %broadcast_compare_fusion) | copy-start | bytes 1179652
  37.8 112.5 %copy-start.10 = (pred[384,1024]{1,0:T(8,128)(4,1)}, pred[384,1024]{1,0:T(8,128)(4,1)S(1)}, u32[]{:S(2)}) copy-start(pred[384,1024]{1,0:T(8,128)(4,1)S(1)} %broadcast_compare_fusion.1) | copy-start | bytes 1179652
  59.0 46.1 %copy-start.37 = (bf16[5,384,64]{1,2,0:T(8,128)(2,1)}, bf16[5,384,64]{1,2,0:T(8,128)(2,1)S(1)}, u32[]{:S(2)}) copy-start(bf16[5,384,64]{1,2,0:T(8,128)(2,1)S(1)} %reshape.569) | copy-start | bytes 737284
  59.6 86.4 %copy-start.35 = (bf16[5,384,64]{1,2,0:T(8,128)(2,1)}, bf16[5,384,64]{1,2,0:T(8,128)(2,1)S(1)}, u32[]{:S(2)}) copy-start(bf16[5,384,64]{1,2,0:T(8,128)(2,1)S(1)} %reshape.564) | copy-start | bytes 737284
  110.2 53.5 %copy-start.29 = (bf16[128,5,3,64]{0,3,2,1:T(8,128)(2,1)}, bf16[128,5,3,64]{0,3,2,1:T(8,128)(2,1)S(1)}, u32[]{:S(2)}) copy-start(bf16[128,5,3,64]{0,3,2,1:T(8,128)(2,1)S(1)} %copy.79) | copy-start | bytes 737284
  152.6 86.0 %copy-start.31 = (bf16[128,5,3,64]{0,3,2,1:T(8,128)(2,1)}, bf16[128,5,3,64]{0,3,2,1:T(8,128)(2,1)S(1)}, u32[]{:S(2)}) copy-start(bf16[128,5,3,64]{0,3,2,1:T(8,128)(2,1)S(1)} %copy.72) | copy-start | bytes 737284
  238.7 33.0 %copy-start.26 = (bf16[2,1,128,960]{2,3,1,0:T(8,128)(2,1)S(1)}, bf16[2,1,128,960]{2,3,1,0:T(8,128)(2,1)}, u32[]{:S(2)}) copy-start(bf16[2,1,128,960]{2,3,1,0:T(8,128)(2,1)} %param.11) | copy-start | bytes 1474564
  315.0 144.2 %reduce-scatter.10.cloned.1.call-start = ((), (), s32[]{:S(2)}) async-start(), calls=%async_computation.14 | async-start | bytes 2949120 | tf_op jit(solution)/shard_map/reduce_scatter | solution.py:271
  317.2 12.3 %slice-start = ((s8[7864320]{0:T(1024)(128)(4,1)}), s8[4194304]{0:T(1024)(128)(4,1)S(1)}, s32[]{:S(2)}) async-start(s8[7864320]{0:T(1024)(128)(4,1)} %bitcast.245), calls=%async_computation.21 | async-start | bytes 8388608
  333.4 178.9 %reduce-scatter.14.cloned.1.call-start = ((), (), s32[]{:S(2)}) async-start(), calls=%async_computation.16 | async-start | bytes 2457600 | tf_op jit(solution)/shard_map/reduce_scatter | solution.py:299
  346.0 179.3 %reduce-scatter.18.cloned.1.call-start = ((), (), s32[]{:S(2)}) async-start(), calls=%async_computation.18 | async-start | bytes 2457600 | tf_op jit(solution)/shard_map/reduce_scatter | solution.py:305
  349.1 204.7 %reduce-scatter.16.cloned.1.call-start = ((), (), s32[]{:S(2)}) async-start(), calls=%async_computation.17 | async-start | bytes 1536000 | tf_op jit(solution)/shard_map/reduce_scatter | solution.py:302
  387.1 76.4 %copy-start.42 = (bf16[128,320]{0,1:T(8,128)(2,1)}, bf16[128,320]{0,1:T(8,128)(2,1)S(1)}, u32[]{:S(2)}) copy-start(bf16[128,320]{0,1:T(8,128)(2,1)S(1)} %slice.310) | copy-start | bytes 245764
  463.5 144.4 %reduce-scatter.22.cloned.1.call-start = ((), (), s32[]{:S(2)}) async-start(), calls=%async_computation.20 | async-start | bytes 6553600
  478.0 213.4 %reduce-scatter.20.cloned.1.call-start = ((), (), s32[]{:S(2)}) async-start(), calls=%async_computation.19 | async-start | bytes 12288000 | tf_op jit(solution)/shard_map/reduce_scatter | solution.py:308
  508.5 16.8 %copy-start.9 = (bf16[960,640]{1,0:T(8,128)(2,1)S(1)}, bf16[960,640]{1,0:T(8,128)(2,1)}, u32[]{:S(2)}) copy-start(bf16[960,640]{1,0:T(8,128)(2,1)} %all-gather.10.cloned.1.call-done) | copy-start | bytes 3686404
  508.5 16.8 %copy-start.43 = (bf16[128,320]{0,1:T(8,128)(2,1)S(1)}, bf16[128,320]{0,1:T(8,128)(2,1)}, u32[]{:S(2)}) copy-start(bf16[128,320]{0,1:T(8,128)(2,1)} %copy-done.42) | copy-start | bytes 245764
  510.8 24.3 %copy-start.62 = (f32[128]{0:T(128)S(1)}, f32[128]{0:T(128)}, u32[]{:S(2)}) copy-start(f32[128]{0:T(128)} %copy-done.61) | copy-start | bytes 1540
  510.8 24.3 %copy-start.64 = (f32[128]{0:T(128)S(1)}, f32[128]{0:T(128)}, u32[]{:S(2)}) copy-start(f32[128]{0:T(128)} %copy-done.63) | copy-start | bytes 1540
  510.8 24.3 %copy-start.17 = (f32[128,960]{0,1:T(8,128)S(1)}, f32[128,960]{0,1:T(8,128)}, u32[]{:S(2)}) copy-start(f32[128,960]{0,1:T(8,128)} %copy-done.15) | copy-start | bytes 1474564
  (52 other events, 216.6 us)
Sparse Core Ops, SparseCore 0:
  9.6 20.4 all-gather.9
  31.6 21.8 all-gather.7
  56.3 42.0 all-gather.19
  101.0 40.6 all-gather.11
  143.1 20.5 all-gather.13
  165.1 66.4 all-gather.15
  233.1 38.5 all-gather.17
  315.1 70.9 reduce-scatter.11
  389.7 69.5 reduce-scatter.9
  462.2 29.5 reduce-scatter.13
  494.6 30.6 reduce-scatter.17
  527.7 26.0 reduce-scatter.15
  556.5 51.3 reduce-scatter.21
  610.4 80.9 reduce-scatter.19
where the time goes:
time: 1090 us; the launch traced here: 1080 us
  waiting for transfers between devices  473 us (43%)
  blocking collectives  400 us (37%)
  matrix products  126 us (12%)
  local copies, waits for them, and re-layouts  40.6 us (4%)
  other arithmetic  27.4 us (3%)
  between operations  17 us (2%)
    psum x1, blocking collectives, local(): lax.psum((owned[0], owned[1], owned[2], owned[3], owned[4], owned[5], own...  386 us
    reduce_scatter x2, waiting for transfers between devices, local(): lax.psum_scatter(dkv_blocks.reshape(seq_len, 2 * kv_width), 'ctx', scatte...  108 us
    reduce_scatter x1, waiting for transfers between devices, local(): lax.psum_scatter(grad_names[5].astype(jnp.bfloat16), 'wt', scatter_dimens...  81.4 us
    all_gather x2, waiting for transfers between devices, local(): kv_whole = lax.all_gather(kv_send, 'ctx', axis=0, tiled=True)  70.2 us
    all_gather x1, waiting for transfers between devices, local(): lax.all_gather(w_gu, 'wt', axis=0, tiled=True)  63 us
    unnamed x15, waiting for transfers between devices  57.4 us
    dot_general x10, matrix products, outer_sum(): lax.dot_general(left, right, (((0,), (0,)), ((), ())), preferred_element_...  35.2 us
    all_gather x1, waiting for transfers between devices, local(): lax.all_gather(w_down, 'wt', axis=0, tiled=True)  29.9 us
  transfers between devices with their start and end apart: 14, of which 13 were waited for; matrix products, arithmetic and copies ran while one was open for 14% of the time, Pallas kernels for 0%

commit v1 on v0

--- a/solution.py
+++ b/solution.py
@@ -9,6 +9,17 @@
 HD = 64
 eps_norm = 1e-05
 rope_base = 10000.0
+
+
+def turned_line(x, name, d):
+    size = lax.axis_size(name)
+    forward = [(i, (i + 1) % size) for i in range(size)]
+    pieces = [x]
+    for far in range(1, size):
+        pieces = [lax.ppermute(pieces[0], name, forward), *pieces]
+    whole = jnp.concatenate(pieces, axis=d)
+    places = (lax.axis_index(name) + 1) * pieces[-1].shape[d]
+    return jnp.roll(whole, places, axis=d)
 
 
 def norm_scale(values, gain):
@@ -141,7 +152,7 @@
             seg_rows, kv_width
         )
         kv_send = jnp.concatenate([key_rot, kv_lin[:, kv_width:]], axis=1).astype(jnp.bfloat16)
-        kv_whole = lax.all_gather(kv_send, "ctx", axis=0, tiled=True)
+        kv_whole = turned_line(kv_send, "ctx", 0)
         kv_blocks = kv_whole.reshape(block_count, key_block, 2 * kv_width)
         pos_blocks = key_pos.reshape(block_count, key_block)
 

time: 1090 us -> 1050 us (0.963)
  waiting for transfers between devices: 473 us -> 401 us
  local copies, waits for them, and re-layouts: 40.6 us -> 65 us
    all_gather x2, waiting for transfers between devices: 70.2 us -> 6.55 us  [local(): lax.all_gather(kv_send, 'ctx', axis=0, tiled=True)]
    ppermute x0 -> x14, waiting for transfers between devices: none -> 55.5 us  [turned_line(): pieces = [lax.ppermute(pieces[0], name, forward), *pieces]]
    all_gather x1, waiting for transfers between devices: 63 us -> 36.6 us  [local(): lax.all_gather(w_gu, 'wt', axis=0, tiled=True)]
    all_gather x1, waiting for transfers between devices: 15.7 us -> 0.01 us  [local(): lax.all_gather(w_q, 'wt', axis=0, tiled=True)]
    slice x0 -> x6, local copies, waits for them, and re-layouts: none -> 14.7 us  [the longest x4 10.3 us: grad_step(): keys_block = kv_block[:, :kv_width].reshape(key_block, KVH, HD)]
    unnamed x147 -> x231, local copies, waits for them, and re-layouts: 17.7 us -> 30.5 us
    dot_general x2 -> x4, matrix products: 3.13 us -> 14.4 us  [block_scores(): jnp.einsum('hrd,khd->hrk', query_groups, keys_block, preferred_element_ty...]
    all_gather x1, waiting for transfers between devices: 11 us -> 0.02 us  [local(): lax.all_gather(w_o, 'wt', axis=0, tiled=True)]
  transfers between devices with their start and end apart: 14 -> 28, of which waited for: 13 -> 22; matrix products, arithmetic and copies ran while one was open for 14% -> 21% of each run, Pallas kernels for 0% -> 0%
where the time goes in v1:
time: 1050 us
  waiting for transfers between devices  401 us (38%)
  blocking collectives  400 us (38%)
  matrix products  132 us (13%)
  local copies, waits for them, and re-layouts  65 us (6%)
  other arithmetic  26.6 us (3%)
  between operations  17.3 us (2%)
    psum x1, blocking collectives, local(): lax.psum((owned[0], owned[1], owned[2], owned[3], owned[4], owned[5], own...  386 us
    reduce_scatter x2, waiting for transfers between devices, local(): lax.psum_scatter(dkv_blocks.reshape(seq_len, 2 * kv_width), 'ctx', scatte...  98.9 us
    reduce_scatter x1, waiting for transfers between devices, local(): lax.psum_scatter(grad_names[5].astype(jnp.bfloat16), 'wt', scatter_dimens...  81.4 us
    unnamed x15, waiting for transfers between devices  57.4 us
    ppermute x14, waiting for transfers between devices, turned_line(): pieces = [lax.ppermute(pieces[0], name, forward), *pieces]  55.5 us
    all_gather x1, waiting for transfers between devices, local(): lax.all_gather(w_gu, 'wt', axis=0, tiled=True)  36.6 us
    dot_general x10, matrix products, outer_sum(): lax.dot_general(left, right, (((0,), (0,)), ((), ())), preferred_element_...  35.1 us
    unnamed x231, local copies, waits for them, and re-layouts  30.5 us
  transfers between devices with their start and end apart: 28, of which 22 were waited for; matrix products, arithmetic and copies ran while one was open for 21% of the time, Pallas kernels for 0%

profile of v1, /device:TPU:0, one launch (start us, length us, event | category | flops | bytes accessed | tf_op | source)
XLA Modules:
  0.0 1046.6 jit_solution(13362910513926880227)
XLA Ops:
  13.1 8.3 all-reduce.6
  24.2 5.9 all-gather.10.cloned.1.call-done
  38.7 5.6 collective-permute-done.7
  47.2 5.6 collective-permute-done.8
  56.7 4.7 collective-permute-done.9
  61.5 4.7 collective-permute-done.2
  66.2 5.0 collective-permute-done.10
  75.5 4.8 collective-permute-done.11
  89.8 4.5 collective-permute-done.5
  94.8 6.8 collective-permute-done.13
  146.5 5.6 fusion.119
  154.3 36.6 %all-gather.14.cloned.1.call-done = bf16[960,5120]{1,0:T(8,128)(2,1)} async-done(((bf16[240,5120]{1,0:T(8,128)(2,1)}), bf16[960,5120]{1,0:T(8,128)(2,1)}) %all-gather.14.cloned.1.call-update) | async-done | bytes 9830416 | tf_op jit(solution)/shard_map/all_gather | solution.py:102
  190.9 7.1 fusion.110
  201.4 29.5 %all-gather.16.cloned.1.call-done = bf16[2560,960]{0,1:T(8,128)(2,1)} async-done(((bf16[640,960]{0,1:T(8,128)(2,1)}), bf16[2560,960]{0,1:T(8,128)(2,1)}) %all-gather.16.cloned.1.call-update) | async-done | bytes 4915216 | tf_op jit(solution)/shard_map/all_gather | solution.py:103
  230.9 5.6 multiply_convert_fusion.3
  236.6 5.4 multiply_convert_fusion.5
  253.6 6.6 multiply_reduce_fusion
  268.7 6.5 all-gather.18.cloned.1.call-done
  282.6 5.7 fusion.118
  289.4 7.0 multiply_reduce_fusion.1
  309.3 4.3 convolution_multiply_fusion.3
  321.2 27.3 %reduce-scatter.12.cloned.1.call-done = f32[128,640]{0,1:T(8,128)} async-done(((f32[1024,640]{0,1:T(8,128)}), f32[128,640]{0,1:T(8,128)}) %reduce-scatter.12.cloned.1.call-update) | async-done | bytes 327696 | tf_op jit(solution)/shard_map/reduce_scatter | solution.py:282
  350.3 71.6 %reduce-scatter.10.cloned.1.call-done = f32[128,640]{0,1:T(8,128)} async-done(((f32[1024,640]{0,1:T(8,128)}), f32[128,640]{0,1:T(8,128)}) %reduce-scatter.10.cloned.1.call-update) | async-done | bytes 327696 | tf_op jit(solution)/shard_map/reduce_scatter | solution.py:282
  432.5 7.9 copy.96
  440.7 9.6 fusion.21
  450.3 11.8 %add_convert_fusion = bf16[960,5120]{1,0:T(8,128)(2,1)} fusion(f32[960,5120]{1,0:T(8,128)} %fusion.21, bf16[128,2560]{1,0:T(8,128)(2,1)} %copy-done.42, bf16[128,2560]{1,0:T(8,128)(2,1)} %copy-done.41, f32[128,960]{0,1:T(8,128)S(1)} %get-tuple-element.305, f32[128]{0:T(128)S(1)} %fusion.92, f32[960]{0:T(1024)S(1)} %convert_element_type.231), kind=kOutput, calls=%fused_computation | convolution fusion | flops 1271111680 | bytes 31297792 | tf_op jit(solution)/shard_map/dot_general | solution.py:75
  474.9 13.0 %reduce-scatter.18.cloned.1.call-done = bf16[240,960]{1,0:T(8,128)(2,1)} async-done(((bf16[960,960]{1,0:T(8,128)(2,1)}), bf16[240,960]{1,0:T(8,128)(2,1)}) %reduce-scatter.18.cloned.1.call-update) | async-done | bytes 460816 | tf_op jit(solution)/shard_map/reduce_scatter | solution.py:316
  491.8 5.7 all-reduce.5
  499.9 16.5 %reduce-scatter.16.cloned.1.call-done = bf16[240,640]{1,0:T(8,128)(2,1)} async-done(((bf16[960,640]{1,0:T(8,128)(2,1)}), bf16[240,640]{1,0:T(8,128)(2,1)}) %reduce-scatter.16.cloned.1.call-update) | async-done | bytes 307216 | tf_op jit(solution)/shard_map/reduce_scatter | solution.py:313
  516.4 54.2 %reduce-scatter.22.cloned.1.call-done = bf16[640,960]{1,0:T(8,128)(2,1)} async-done(((bf16[2560,960]{1,0:T(8,128)(2,1)}), bf16[640,960]{1,0:T(8,128)(2,1)}) %reduce-scatter.22.cloned.1.call-update) | async-done | bytes 1228816
  572.7 81.4 %reduce-scatter.20.cloned.1.call-done = bf16[240,5120]{1,0:T(8,128)(2,1)} async-done(((bf16[960,5120]{1,0:T(8,128)(2,1)}), bf16[240,5120]{1,0:T(8,128)(2,1)}) %reduce-scatter.20.cloned.1.call-update) | async-done | bytes 2457616 | tf_op jit(solution)/shard_map/reduce_scatter | solution.py:319
  654.1 385.7 %all-reduce.8 = (f32[240]{0:T(256)}, f32[240]{0:T(256)}, f32[240,960]{1,0:T(8,128)}, f32[240,640]{1,0:T(8,128)}, f32[240,960]{1,0:T(8,128)}, /*index=5*/f32[240,5120]{1,0:T(8,128)}, f32[640,960]{0,1:T(8,128)}) all-reduce(f32[240]{0:T(256)S(1)} %get-tuple-element.319, ...), channel_id=1, replica_groups=mesh['ctx'=8,'wt'=4] {'ctx'}, use_global_device_ids=true, to_apply=%region_19.21 | all-reduce | flops 2458080 | bytes 14749440 | tf_op jit(solution)/shard_map/psum | solution.py:326
  (424 shorter events, 168.7 us)
Async XLA Ops:
  7.2 22.9 %all-gather.10.cloned.1.call-start = ((), (), s32[]{:S(2)}) async-start(), calls=%async_computation.8 | async-start | bytes 1536000 | tf_op jit(solution)/shard_map/all_gather | solution.py:100
  7.9 75.8 %all-gather.8.cloned.1.call-start = ((), (), s32[]{:S(2)}) async-start(), calls=%async_computation.7 | async-start | bytes 2457600 | tf_op jit(solution)/shard_map/all_gather | solution.py:99
  8.7 111.3 %all-gather.12.cloned.1.call-start = ((), (), s32[]{:S(2)}) async-start(), calls=%async_computation.9 | async-start | bytes 2457600 | tf_op jit(solution)/shard_map/all_gather | solution.py:101
  9.4 132.0 %all-gather.20.cloned.1.call-start = ((), (), s32[]{:S(2)}) async-start(), calls=%async_computation.14 | async-start | bytes 1474560 | tf_op jit(solution)/shard_map/all_gather | solution.py:227
  33.3 157.7 %all-gather.14.cloned.1.call-start = ((), (), s32[]{:S(2)}) async-start(), calls=%async_computation.10 | async-start | bytes 12288000 | tf_op jit(solution)/shard_map/all_gather | solution.py:102
  33.9 197.0 %all-gather.16.cloned.1.call-start = ((), (), s32[]{:S(2)}) async-start(), calls=%async_computation.11 | async-start | bytes 6144000 | tf_op jit(solution)/shard_map/all_gather | solution.py:103
  34.5 240.7 %all-gather.18.cloned.1.call-start = ((), (), s32[]{:S(2)}) async-start(), calls=%async_computation.12 | async-start | bytes 1474560 | tf_op jit(solution)/shard_map/all_gather | solution.py:227
  34.5 9.8 collective-permute-start.7
  37.2 10.0 collective-permute-start
  44.3 8.5 collective-permute-start.8
  47.1 9.3 collective-permute-start.1
  52.8 8.7 collective-permute-start.9
  56.4 9.7 collective-permute-start.2
  61.5 9.7 collective-permute-start.10
  66.2 8.9 collective-permute-start.3
  71.2 9.2 collective-permute-start.11
  75.1 8.6 collective-permute-start.4
  75.5 273.0 %reduce-scatter.12.cloned.1.call-start = ((), (), s32[]{:S(2)}) async-start(), calls=%async_computation.15 | async-start | bytes 2949120 | tf_op jit(solution)/shard_map/reduce_scatter | solution.py:282
  80.4 8.3 collective-permute-start.12
  83.7 10.6 %collective-permute-start.5 = (bf16[128,640]{1,0:T(8,128)(2,1)}, bf16[128,640]{1,0:T(8,128)(2,1)}, u32[]{:S(2)}, u32[]{:S(2)}) collective-permute-start(bf16[128,640]{1,0:T(8,128)(2,1)} %collective-permute-done.4), channel_id=1, source_target_pairs={{0,4},{4,8},{8,12},{12,16},{16,20},{20,24},{24,28},{28,0},{1,5},{5... | collective-permute-start | bytes 491528 | tf_op jit(solution)/shard_map/ppermute | solution.py:19
  88.7 12.9 %collective-permute-start.13 = (bf16[128,640]{1,0:T(8,128)(2,1)}, bf16[128,640]{1,0:T(8,128)(2,1)}, u32[]{:S(2)}, u32[]{:S(2)}) collective-permute-start(bf16[128,640]{1,0:T(8,128)(2,1)} %collective-permute-done.12), channel_id=1, source_target_pairs={{0,4},{4,8},{8,12},{12,16},{16,20},{20,24},{24,28},{28,0},{1,5},{5... | collective-permute-start | bytes 491528 | tf_op jit(solution)/shard_map/ppermute | solution.py:19
  94.3 28.2 %collective-permute-start.6 = (bf16[128,640]{1,0:T(8,128)(2,1)}, bf16[128,640]{1,0:T(8,128)(2,1)}, u32[]{:S(2)}, u32[]{:S(2)}) collective-permute-start(bf16[128,640]{1,0:T(8,128)(2,1)} %collective-permute-done.5), channel_id=1, source_target_pairs={{0,4},{4,8},{8,12},{12,16},{16,20},{20,24},{24,28},{28,0},{1,5},{5... | collective-permute-start | bytes 491528 | tf_op jit(solution)/shard_map/ppermute | solution.py:19
  268.6 153.3 %reduce-scatter.10.cloned.1.call-start = ((), (), s32[]{:S(2)}) async-start(), calls=%async_computation.13 | async-start | bytes 2949120 | tf_op jit(solution)/shard_map/reduce_scatter | solution.py:282
  304.5 170.4 %reduce-scatter.14.cloned.1.call-start = ((), (), s32[]{:S(2)}) async-start(), calls=%async_computation.16 | async-start | bytes 2457600 | tf_op jit(solution)/shard_map/reduce_scatter | solution.py:310
  318.1 169.9 %reduce-scatter.18.cloned.1.call-start = ((), (), s32[]{:S(2)}) async-start(), calls=%async_computation.18 | async-start | bytes 2457600 | tf_op jit(solution)/shard_map/reduce_scatter | solution.py:316
  321.1 103.4 %copy-start.84 = (f32[128]{0:T(128)S(1)}, f32[128]{0:T(128)}, u32[]{:S(2)}) copy-start(f32[128]{0:T(128)} %copy-done.82) | copy-start | bytes 1540
  321.1 195.3 %reduce-scatter.16.cloned.1.call-start = ((), (), s32[]{:S(2)}) async-start(), calls=%async_computation.17 | async-start | bytes 1536000 | tf_op jit(solution)/shard_map/reduce_scatter | solution.py:313
  426.2 144.4 %reduce-scatter.22.cloned.1.call-start = ((), (), s32[]{:S(2)}) async-start(), calls=%async_computation.20 | async-start | bytes 6553600
  440.5 213.6 %reduce-scatter.20.cloned.1.call-start = ((), (), s32[]{:S(2)}) async-start(), calls=%async_computation.19 | async-start | bytes 12288000 | tf_op jit(solution)/shard_map/reduce_scatter | solution.py:319
  499.1 155.0 %copy-start.49 = (bf16[240,960]{1,0:T(8,128)(2,1)S(1)}, bf16[240,960]{1,0:T(8,128)(2,1)}, u32[]{:S(2)}) copy-start(bf16[240,960]{1,0:T(8,128)(2,1)} %reduce-scatter.14.cloned.1.call-done) | copy-start | bytes 1382404
  499.1 155.0 %copy-start.50 = (bf16[240,960]{1,0:T(8,128)(2,1)S(1)}, bf16[240,960]{1,0:T(8,128)(2,1)}, u32[]{:S(2)}) copy-start(bf16[240,960]{1,0:T(8,128)(2,1)} %reduce-scatter.18.cloned.1.call-done) | copy-start | bytes 1382404
  516.4 137.7 %copy-start.70 = (bf16[240,640]{1,0:T(8,128)(2,1)S(1)}, bf16[240,640]{1,0:T(8,128)(2,1)}, u32[]{:S(2)}) copy-start(bf16[240,640]{1,0:T(8,128)(2,1)} %reduce-scatter.16.cloned.1.call-done) | copy-start | bytes 921604
  (101 other events, 1382.6 us)
Sparse Core Ops, SparseCore 0:
  9.6 20.4 all-gather.9
  31.6 21.8 all-gather.7
  55.1 21.8 all-gather.11
  79.6 44.5 all-gather.19
  125.6 65.3 all-gather.13
  192.4 38.5 all-gather.15
  233.1 42.0 all-gather.17
  278.7 69.7 reduce-scatter.11
  352.0 69.8 reduce-scatter.9
  424.9 29.5 reduce-scatter.13
  457.2 30.6 reduce-scatter.17
  490.4 26.0 reduce-scatter.15
  519.1 51.4 reduce-scatter.21
  573.1 80.9 reduce-scatter.19
